TPU v7x, 128 devices: a whole 4x4x4 slice. The times are simulated.
128 devices in a mesh: group: 8 (over x, core), sub: 16 (over z, y).
Axes of the slice: x: 4, y: 4, z: 4, core: 2. Of those that a mesh axis runs over, the one named last changes fastest.
Arguments:
- schur: bfloat16 [8, 16, 1024, 1024], P('group', 'sub'), as said below
- local_inverse: bfloat16 [8, 16, 1024, 1024], P('group', 'sub'), as said below
- rhs_parts: bfloat16 [8, 16, 1024, 128], P('group', 'sub'), may hold values from -6 to 6
- basis: bfloat16 [8, 16, 32, 1024], P('group', 'sub'), may hold values from -0.1875 to 0.1875
- coarse_map: int32 [8, 16, 32], P('group', 'sub'), may hold values from 0 to 1023
- coarse_inverse: bfloat16 [8, 1024, 1024], P('group', 'sub'), as said below
- shared_rows: int32 [8, 16, 2, 4, 256], P('group', 'sub'), may hold values from 0 to 1023, as said below
- shared_counts: int32 [8, 16, 4], P('group', 'sub'), may hold values from 0 to 256, as said below
Outputs:
- solution: float32 [8, 16, 1024, 128], P('group', 'sub')
- residual: float32 [8, 16, 1024, 128], P('group', 'sub')
Inputs may be any that keep to these rules, and one draw needn't show every extreme that they name: `schur`: each subdomain matrix is symmetric positive definite. `local_inverse`: each subdomain matrix is symmetric positive definite. `coarse_inverse`: each group's matrix is symmetric positive definite. `shared_rows`: own rows of direction d lie in rows d * 256 to (d + 1) * 256 - 1 and are distinct within a list; the own rows of direction 0 of (g, s) are the partner rows of direction 1 of (g, s + 1) and the reverse, likewise directions 2 and 3 between (g, s) and (g + 1, s); entries past the count are rows of the same block. `shared_counts`: the count of direction 0 of (g, s) equals the count of direction 1 of (g, s + 1), that of direction 2 of (g, s) the count of direction 3 of (g + 1, s); counts are 0 where no neighbour exists; some count equals 256.
All inputs are finite; a program needn't handle non-finite values.
Results may differ from a plain program's by a relative error of at most 0.014.
Values may be sent and summed in bfloat16 or wider, within the bound.
A program may use at most 64 MiB of HBM per device.

v0:
```python
import jax
import jax.numpy as jnp
from jax import lax
from jax.sharding import PartitionSpec as P

ITERS = 3


def extended(block, sides, width):
    for axis, dim in sides:
        count = lax.axis_size(axis)
        forward = [(i, i + 1) for i in range(count - 1)]
        backward = [(target, source) for source, target in forward]
        low = lax.ppermute(
            lax.slice_in_dim(block, block.shape[dim] - width, None, axis=dim), axis, forward
        )
        high = lax.ppermute(lax.slice_in_dim(block, 0, width, axis=dim), axis, backward)
        block = jnp.concatenate([low, block, high], axis=dim)
    return block


def pick_rows(tables, indices):
    return jax.vmap(jax.vmap(lambda source_block, rows_at: source_block[rows_at]))(tables, indices)


def add_rows(bases, indices, additions):

    def add_single(base_block, rows_at, extra):
        return base_block.at[rows_at.reshape(-1)].add(extra.reshape(-1, base_block.shape[-1]))

    return jax.vmap(jax.vmap(add_single))(bases, indices, additions)


def count_rows(indices, live_mask, rows_local):

    def count_single(rows_at, mask_rows):
        return (
            jnp.ones((rows_local,), jnp.float32).at[rows_at.reshape(-1)].add(mask_rows.reshape(-1))
        )

    return jax.vmap(jax.vmap(count_single))(indices, live_mask)


def assemble(blocks, own_rows, partner_rows, live_mask):
    padded = extended(blocks, (("group", 0), ("sub", 1)), 1)
    received = jnp.stack(
        [
            pick_rows(padded[1:2, 2:], partner_rows[:, :, 0]),
            pick_rows(padded[1:2, :-2], partner_rows[:, :, 1]),
            pick_rows(padded[2:3, 1:-1], partner_rows[:, :, 2]),
            pick_rows(padded[0:1, 1:-1], partner_rows[:, :, 3]),
        ],
        axis=2,
    )
    values = received * live_mask[..., None]
    return add_rows(blocks, own_rows, values)


def gram_matrix(left, right, weight):
    local_gram = jnp.einsum(
        "gsir,gsic->rc", left * weight[..., None], right, precision=lax.Precision.HIGHEST
    )
    return lax.psum(local_gram, ("group", "sub"))


def spd_solve(matrix, rhs_block):
    factor = jnp.linalg.cholesky(matrix)
    half = lax.linalg.triangular_solve(factor, rhs_block, left_side=True, lower=True)
    return lax.linalg.triangular_solve(factor, half, left_side=True, lower=True, transpose_a=True)


def contract(blocks, mixing):
    return jnp.einsum("gsir,rc->gsic", blocks, mixing, precision=lax.Precision.HIGHEST)


def shards(
    schur, local_inverse, rhs_parts, basis, coarse_map, coarse_inverse, shared_rows, shared_counts
):
    capacity = shared_rows.shape[-1]
    rows_local = rhs_parts.shape[2]
    columns = rhs_parts.shape[3]
    coarse_total = coarse_inverse.shape[2]
    live_mask = (jnp.arange(capacity, dtype=jnp.int32) < shared_counts[..., None]).astype(
        jnp.float32
    )
    own_rows = shared_rows[:, :, 0]
    partner_rows = shared_rows[:, :, 1]
    weight = 1.0 / count_rows(own_rows, live_mask, rows_local)
    selector = (
        coarse_map.reshape(-1)[:, None] == jnp.arange(coarse_total, dtype=jnp.int32)[None, :]
    ).astype(jnp.float32)
    selector_half = selector.astype(jnp.bfloat16)
    full_inverse = coarse_inverse[0]

    def precondition(resid):
        scaled = (weight[..., None] * resid).astype(jnp.bfloat16)
        local_part = jnp.einsum(
            "gsij,gsjr->gsir", local_inverse, scaled, preferred_element_type=jnp.float32
        )
        coarse_local = jnp.einsum(
            "gsmi,gsir->gsmr", basis, scaled, preferred_element_type=jnp.float32
        )
        contrib = jnp.dot(
            selector.T, coarse_local.reshape(-1, columns), precision=lax.Precision.HIGHEST
        )
        coarse_residual = lax.psum(contrib, "sub")
        coarse_rounded = coarse_residual.astype(jnp.bfloat16)
        row_values = jnp.dot(
            full_inverse, coarse_rounded, preferred_element_type=jnp.float32
        ).astype(jnp.bfloat16)
        coarse_values = lax.all_gather(row_values, "sub", axis=0, tiled=True)
        picked = (
            jnp.dot(selector_half, coarse_values, preferred_element_type=jnp.float32)
            .astype(jnp.bfloat16)
            .reshape(coarse_local.shape)
        )
        coarse_part = jnp.einsum(
            "gsmi,gsmr->gsir", basis, picked, preferred_element_type=jnp.float32
        )
        smoothed = weight[..., None] * (local_part + coarse_part)
        return assemble(smoothed, own_rows, partner_rows, live_mask)

    residual = assemble(rhs_parts.astype(jnp.float32), own_rows, partner_rows, live_mask)
    solution = jnp.zeros_like(residual)
    precond = precondition(residual)
    direction = precond
    inner = gram_matrix(precond, residual, weight)
    for iteration in range(ITERS):
        local_image = jnp.einsum(
            "gsij,gsjr->gsir",
            schur,
            direction.astype(jnp.bfloat16),
            preferred_element_type=jnp.float32,
        )
        image = assemble(local_image, own_rows, partner_rows, live_mask)
        curvature = gram_matrix(direction, image, weight)
        step_size = spd_solve(curvature, inner)
        solution = solution + contract(direction, step_size)
        residual = residual - contract(image, step_size)
        if iteration + 1 < ITERS:
            precond = precondition(residual)
            inner_next = gram_matrix(precond, residual, weight)
            conjugacy = spd_solve(inner, inner_next)
            direction = precond + contract(direction, conjugacy)
            inner = inner_next
    return (solution, residual)


def solution(mesh):
    placed = (
        P("group", "sub", None, None),
        P("group", "sub", None, None),
        P("group", "sub", None, None),
        P("group", "sub", None, None),
        P("group", "sub", None),
        P("group", "sub", None),
        P("group", "sub", None, None, None),
        P("group", "sub", None),
    )
    return jax.shard_map(
        shards,
        mesh=mesh,
        in_specs=placed,
        out_specs=(P("group", "sub", None, None), P("group", "sub", None, None)),
        check_vma=False,
    )
```

profile of v0, /device:TPU:1, one launch (start us, length us, event | category | flops | bytes accessed | tf_op | source)
XLA Modules:
  0.0 1686.3 jit_solution(6008829933205526659)
XLA Ops:
  9.2 4.5 collective-permute-start
  20.1 4.4 collective-permute-done.1
  26.9 4.4 collective-permute-start.3
  32.6 7.6 scatter_custom_fusion
  44.1 14.3 collective-permute-done.3
  68.9 6.7 scatter_custom_fusion.1
  78.5 66.6 %all-reduce.19 = bf16[1024,128]{1,0:T(8,128)(2,1)} all-reduce(f32[1024,128]{1,0:T(8,128)S(1)} %fusion.81), channel_id=1, replica_groups=mesh['group'=8,'sub'=16] {'sub'}, use_global_device_ids=true, to_apply=%region_2.0 | all-reduce | flops 131072 | bytes 786432 | tf_op jit(solution)/shard_map/psum | solution.py:106
  146.2 18.0 %all_gather.9 = bf16[1024,128]{1,0:T(8,128)(2,1)} all-gather(bf16[64,128]{1,0:T(8,128)(2,1)S(1)} %fusion.21), channel_id=1, replica_groups=mesh['group'=8,'sub'=16] {'sub'}, dimensions={0}, use_global_device_ids=true | all-gather | bytes 278528 | tf_op jit(solution)/shard_map/all_gather | solution.py:111
  165.8 27.7 %collective-permute-start.4 = (f32[1,1,1024,128]{2,3,1,0:T(8,128)S(1)}, f32[1,1,1024,128]{2,3,1,0:T(8,128)S(1)}, u32[]{:S(2)}, u32[]{:S(2)}) collective-permute-start(f32[1,1,1024,128]{2,3,1,0:T(8,128)S(1)} %bitcast.401), channel_id=1, source_target_pairs={{0,16},{16,32},{32,48},{48,64},{64,80},{80,96},{96,112},{1,17},{17... | collective-permute-start | bytes 1572872 | tf_op jit(solution)/shard_map/ppermute | solution.py:14
  195.5 4.2 collective-permute-done.4
  199.7 4.4 collective-permute-done.5
  205.4 4.6 collective-permute-start.7
  219.2 3.0 gather_fusion.6
  222.3 14.5 collective-permute-done.7
  240.6 3.0 gather_fusion.5
  247.6 3.1 gather_fusion.4
  252.7 6.7 scatter_custom_fusion.2
  261.9 8.1 collective-permute-start.8
  271.9 4.2 collective-permute-done.8
  276.1 4.4 collective-permute-done.9
  281.8 5.7 collective-permute-start.11
  298.6 15.6 collective-permute-done.11
  326.6 7.1 scatter_custom_fusion.3
  335.6 149.4 %all-reduce.18.cloned.1.call-done = (f32[128,128]{0,1:T(8,128)}, f32[128,128]{0,1:T(8,128)}) async-done(((f32[128,128]{0,1:T(8,128)}, f32[128,128]{0,1:T(8,128)}), (f32[128,128]{0,1:T(8,128)}, f32[128,128]{0,1:T(8,128)})) %all-reduce.18.cloned.1.call-update) | async-done | bytes 131088 | tf_op jit(solution)/shard_map/psum | solution.py:63
  488.4 12.5 cholesky.89
  502.3 9.8 custom-call.73
  518.9 64.9 %all-reduce.20 = bf16[1024,128]{1,0:T(8,128)(2,1)} all-reduce(f32[1024,128]{1,0:T(8,128)} %fusion.80), channel_id=1, replica_groups=mesh['group'=8,'sub'=16] {'sub'}, use_global_device_ids=true, to_apply=%region_9.13 | all-reduce | flops 131072 | bytes 786432 | tf_op jit(solution)/shard_map/psum | solution.py:106
  584.9 18.3 %all_gather.10 = bf16[1024,128]{1,0:T(8,128)(2,1)} all-gather(bf16[64,128]{1,0:T(8,128)(2,1)S(1)} %fusion.22), channel_id=1, replica_groups=mesh['group'=8,'sub'=16] {'sub'}, dimensions={0}, use_global_device_ids=true | all-gather | bytes 278528 | tf_op jit(solution)/shard_map/all_gather | solution.py:111
  605.6 21.6 %collective-permute-start.12 = (f32[1,1,1024,128]{2,3,1,0:T(8,128)}, f32[1,1,1024,128]{2,3,1,0:T(8,128)S(1)}, u32[]{:S(2)}, u32[]{:S(2)}) collective-permute-start(f32[1,1,1024,128]{2,3,1,0:T(8,128)} %bitcast.405), channel_id=1, source_target_pairs={{0,16},{16,32},{32,48},{48,64},{64,80},{80,96},{96,112},{1,17},{17... | collective-permute-start | bytes 1572872 | tf_op jit(solution)/shard_map/ppermute | solution.py:14
  629.1 4.5 collective-permute-done.12
  633.6 4.3 collective-permute-done.13
  640.4 4.2 collective-permute-start.15
  647.9 12.5 cholesky.100
  663.2 3.1 gather_fusion.15
  687.6 8.2 scatter_custom_fusion.4
  699.7 9.8 custom-call.75
  709.5 135.7 %all-reduce.10.cloned.1.call-done = f32[128,128]{0,1:T(8,128)} async-done(((f32[128,128]{0,1:T(8,128)}), f32[128,128]{0,1:T(8,128)}) %all-reduce.10.cloned.1.call-update) | async-done | bytes 65552 | tf_op jit(solution)/shard_map/psum | solution.py:63
  854.9 4.2 collective-permute-done.16
  859.1 4.4 collective-permute-done.17
  864.8 4.1 collective-permute-start.19
  874.3 3.1 gather_fusion.19
  882.4 13.5 collective-permute-done.19
  911.8 8.3 scatter_custom_fusion.5
  923.4 144.1 %all-reduce.12.cloned.1.call-done = f32[128,128]{0,1:T(8,128)} async-done(((f32[128,128]{0,1:T(8,128)}), f32[128,128]{0,1:T(8,128)}) %all-reduce.12.cloned.1.call-update) | async-done | bytes 65552 | tf_op jit(solution)/shard_map/psum | solution.py:63
  1070.6 13.2 cholesky.111
  1087.4 11.3 custom-call.77
  1107.0 64.4 %all-reduce.21 = bf16[1024,128]{1,0:T(8,128)(2,1)} all-reduce(f32[1024,128]{1,0:T(8,128)} %fusion.79), channel_id=1, replica_groups=mesh['group'=8,'sub'=16] {'sub'}, use_global_device_ids=true, to_apply=%region_14.18 | all-reduce | flops 131072 | bytes 786432 | tf_op jit(solution)/shard_map/psum | solution.py:106
  1172.4 18.2 %all_gather.11 = bf16[1024,128]{1,0:T(8,128)(2,1)} all-gather(bf16[64,128]{1,0:T(8,128)(2,1)S(1)} %fusion.23), channel_id=1, replica_groups=mesh['group'=8,'sub'=16] {'sub'}, dimensions={0}, use_global_device_ids=true | all-gather | bytes 278528 | tf_op jit(solution)/shard_map/all_gather | solution.py:111
  1193.0 21.2 %collective-permute-start.20 = (f32[1,1,1024,128]{2,3,1,0:T(8,128)}, f32[1,1,1024,128]{2,3,1,0:T(8,128)S(1)}, u32[]{:S(2)}, u32[]{:S(2)}) collective-permute-start(f32[1,1,1024,128]{2,3,1,0:T(8,128)} %bitcast.397), channel_id=1, source_target_pairs={{0,16},{16,32},{32,48},{48,64},{64,80},{80,96},{96,112},{1,17},{17... | collective-permute-start | bytes 1572872 | tf_op jit(solution)/shard_map/ppermute | solution.py:14
  1216.1 4.5 collective-permute-done.20
  1220.6 4.3 collective-permute-done.21
  1227.4 4.2 collective-permute-start.23
  1233.2 11.7 cholesky.122
  1274.6 8.2 scatter_custom_fusion.6
  1286.7 9.8 custom-call.79
  1296.5 134.3 %all-reduce.14.cloned.1.call-done = f32[128,128]{1,0:T(8,128)} async-done(((f32[128,128]{1,0:T(8,128)}), f32[128,128]{1,0:T(8,128)}) %all-reduce.14.cloned.1.call-update) | async-done | bytes 65552 | tf_op jit(solution)/shard_map/psum | solution.py:63
  1440.8 4.2 collective-permute-done.24
  1445.0 4.4 collective-permute-done.25
  1450.7 4.1 collective-permute-start.27
  1464.9 16.9 %collective-permute-done.27 = f32[3,1,1024,128]{2,3,1,0:T(8,128)} collective-permute-done((f32[3,1,1024,128]{2,3,1,0:T(8,128)}, f32[3,1,1024,128]{2,3,1,0:T(8,128)}, u32[]{:S(2)}, u32[]{:S(2)}) %collective-permute-start.27) | collective-permute-done | bytes 1572896 | tf_op jit(solution)/shard_map/ppermute | solution.py:14
  1494.4 8.5 scatter_custom_fusion.7
  1508.2 142.2 %all-reduce.16.cloned.1.call-done = f32[128,128]{0,1:T(8,128)} async-done(((f32[128,128]{0,1:T(8,128)}), f32[128,128]{0,1:T(8,128)}) %all-reduce.16.cloned.1.call-update) | async-done | bytes 65552 | tf_op jit(solution)/shard_map/psum | solution.py:63
  1652.2 11.7 cholesky.133
  1665.2 9.8 custom-call.81
  (281 shorter events, 281.1 us)
Async XLA Ops:
  7.2 68.4 %copy-start = (bf16[1,1,1024,1024]{3,2,1,0:T(8,128)(2,1)S(1)}, bf16[1,1,1024,1024]{3,2,1,0:T(8,128)(2,1)}, u32[]{:S(2)}) copy-start(bf16[1,1,1024,1024]{3,2,1,0:T(8,128)(2,1)} %param.14) | copy-start | bytes 6291460
  7.2 477.8 %all-reduce.18.cloned.1.call-start = ((), (), s32[]{:S(2)}) async-start(), calls=%async_computation.4 | async-start | bytes 262144 | tf_op jit(solution)/shard_map/psum | solution.py:63
  9.2 10.9 collective-permute-start
  13.7 10.8 collective-permute-start.1
  26.9 31.5 %collective-permute-start.3 = (f32[3,1,1024,128]{3,2,1,0:T(8,128)}, f32[3,1,1024,128]{3,2,1,0:T(8,128)}, u32[]{:S(2)}, u32[]{:S(2)}) collective-permute-start(f32[3,1,1024,128]{3,2,1,0:T(8,128)} %pad_maximum_fusion), channel_id=1, source_target_pairs={{0,1},{1,2},{2,3},{3,4},{4,5},{5,6},{6,7},{7,8},{8,9},{9,10},{10,1... | collective-permute-start | bytes 4718600 | tf_op jit(solution)/shard_map/ppermute | solution.py:14
  31.3 32.4 %collective-permute-start.2 = (f32[3,1,1024,128]{3,2,1,0:T(8,128)}, f32[3,1,1024,128]{3,2,1,0:T(8,128)}, u32[]{:S(2)}, u32[]{:S(2)}) collective-permute-start(f32[3,1,1024,128]{3,2,1,0:T(8,128)} %pad_maximum_fusion), channel_id=1, source_target_pairs={{1,0},{2,1},{3,2},{4,3},{5,4},{6,5},{7,6},{8,7},{9,8},{10,9},{11,1... | collective-permute-start | bytes 4718600 | tf_op jit(solution)/shard_map/ppermute | solution.py:17
  75.5 215.2 %copy-start.4 = (f32[1024,128]{1,0:T(8,128)}, f32[1024,128]{1,0:T(8,128)S(1)}, u32[]{:S(2)}) copy-start(f32[1024,128]{1,0:T(8,128)S(1)} %scatter_custom_fusion.1) | copy-start | bytes 1572868
  75.6 1.9 copy-start.14
  75.6 2.2 copy-start.33
  77.4 67.6 %copy-start.28 = (bf16[1,64,1024]{2,1,0:T(8,128)(2,1)S(1)}, bf16[1,64,1024]{2,1,0:T(8,128)(2,1)}, u32[]{:S(2)}) copy-start(bf16[1,64,1024]{2,1,0:T(8,128)(2,1)} %param.18) | copy-start | bytes 393220
  165.8 39.6 %copy-start.10 = (f32[128,1024]{1,0:T(8,128)}, f32[128,1024]{1,0:T(8,128)S(1)}, u32[]{:S(2)}) copy-start(f32[128,1024]{1,0:T(8,128)S(1)} %fusion.12) | copy-start | bytes 1572868
  165.8 33.9 %collective-permute-start.4 = (f32[1,1,1024,128]{2,3,1,0:T(8,128)S(1)}, f32[1,1,1024,128]{2,3,1,0:T(8,128)S(1)}, u32[]{:S(2)}, u32[]{:S(2)}) collective-permute-start(f32[1,1,1024,128]{2,3,1,0:T(8,128)S(1)} %bitcast.401), channel_id=1, source_target_pairs={{0,16},{16,32},{32,48},{48,64},{64,80},{80,96},{96,112},{1,17},{17... | collective-permute-start | bytes 1572872 | tf_op jit(solution)/shard_map/ppermute | solution.py:14
  193.6 10.5 collective-permute-start.5
  199.7 5.7 copy-start.24
  205.4 31.3 %collective-permute-start.7 = (f32[3,1,1024,128]{2,3,1,0:T(8,128)}, f32[3,1,1024,128]{2,3,1,0:T(8,128)}, u32[]{:S(2)}, u32[]{:S(2)}) collective-permute-start(f32[3,1,1024,128]{2,3,1,0:T(8,128)} %pad_maximum_fusion.1), channel_id=1, source_target_pairs={{0,1},{1,2},{2,3},{3,4},{4,5},{5,6},{6,7},{7,8},{8,9},{9,10},{10,1... | collective-permute-start | bytes 4718600 | tf_op jit(solution)/shard_map/ppermute | solution.py:14
  210.0 33.7 %collective-permute-start.6 = (f32[3,1,1024,128]{2,3,1,0:T(8,128)}, f32[3,1,1024,128]{2,3,1,0:T(8,128)}, u32[]{:S(2)}, u32[]{:S(2)}) collective-permute-start(f32[3,1,1024,128]{2,3,1,0:T(8,128)} %pad_maximum_fusion.1), channel_id=1, source_target_pairs={{1,0},{2,1},{3,2},{4,3},{5,4},{6,5},{7,6},{8,7},{9,8},{10,9},{11,1... | collective-permute-start | bytes 4718600 | tf_op jit(solution)/shard_map/ppermute | solution.py:17
  261.8 20.0 %copy-start.12 = (f32[128,1024]{1,0:T(8,128)}, f32[128,1024]{1,0:T(8,128)S(1)}, u32[]{:S(2)}) copy-start(f32[128,1024]{1,0:T(8,128)S(1)} %fusion.4) | copy-start | bytes 1572868
  261.9 14.2 collective-permute-start.8
  269.9 10.5 collective-permute-start.9
  276.1 5.7 copy-start.22
  280.4 1.4 copy-start.23
  281.8 32.4 %collective-permute-start.11 = (f32[3,1,1024,128]{2,3,1,0:T(8,128)}, f32[3,1,1024,128]{2,3,1,0:T(8,128)}, u32[]{:S(2)}, u32[]{:S(2)}) collective-permute-start(f32[3,1,1024,128]{2,3,1,0:T(8,128)} %pad_maximum_fusion.2), channel_id=1, source_target_pairs={{0,1},{1,2},{2,3},{3,4},{4,5},{5,6},{6,7},{7,8},{8,9},{9,10},{10,1... | collective-permute-start | bytes 4718600 | tf_op jit(solution)/shard_map/ppermute | solution.py:14
  287.5 32.0 %collective-permute-start.10 = (f32[3,1,1024,128]{2,3,1,0:T(8,128)}, f32[3,1,1024,128]{2,3,1,0:T(8,128)}, u32[]{:S(2)}, u32[]{:S(2)}) collective-permute-start(f32[3,1,1024,128]{2,3,1,0:T(8,128)} %pad_maximum_fusion.2), channel_id=1, source_target_pairs={{1,0},{2,1},{3,2},{4,3},{5,4},{6,5},{7,6},{8,7},{9,8},{10,9},{11,1... | collective-permute-start | bytes 4718600 | tf_op jit(solution)/shard_map/ppermute | solution.py:17
  321.5 5.1 copy-start.8
  333.7 179.5 %copy-start.9 = (f32[1024,128]{1,0:T(8,128)}, f32[1024,128]{1,0:T(8,128)S(1)}, u32[]{:S(2)}) copy-start(f32[1024,128]{1,0:T(8,128)S(1)} %scatter_custom_fusion.3) | copy-start | bytes 1572868
  335.5 509.6 %all-reduce.10.cloned.1.call-start = ((), (), s32[]{:S(2)}) async-start(), calls=%async_computation | async-start | bytes 131072 | tf_op jit(solution)/shard_map/psum | solution.py:63
  515.2 180.6 %copy-start.3 = (f32[1,1,1024,128]{3,2,1,0:T(8,128)}, f32[1,1,1024,128]{3,2,1,0:T(8,128)S(1)}, u32[]{:S(2)}) copy-start(f32[1,1,1024,128]{3,2,1,0:T(8,128)S(1)} %fusion.16) | copy-start | bytes 1572868
  605.6 28.0 %collective-permute-start.12 = (f32[1,1,1024,128]{2,3,1,0:T(8,128)}, f32[1,1,1024,128]{2,3,1,0:T(8,128)S(1)}, u32[]{:S(2)}, u32[]{:S(2)}) collective-permute-start(f32[1,1,1024,128]{2,3,1,0:T(8,128)} %bitcast.405), channel_id=1, source_target_pairs={{0,16},{16,32},{32,48},{48,64},{64,80},{80,96},{96,112},{1,17},{17... | collective-permute-start | bytes 1572872 | tf_op jit(solution)/shard_map/ppermute | solution.py:14
  627.1 10.7 collective-permute-start.13
  633.6 6.8 copy-start.18
  637.9 2.5 copy-start.19
  640.4 31.3 %collective-permute-start.15 = (f32[3,1,1024,128]{2,3,1,0:T(8,128)}, f32[3,1,1024,128]{2,3,1,0:T(8,128)}, u32[]{:S(2)}, u32[]{:S(2)}) collective-permute-start(f32[3,1,1024,128]{2,3,1,0:T(8,128)} %pad_maximum_fusion.3), channel_id=1, source_target_pairs={{0,1},{1,2},{2,3},{3,4},{4,5},{5,6},{6,7},{7,8},{8,9},{9,10},{10,1... | collective-permute-start | bytes 4718600 | tf_op jit(solution)/shard_map/ppermute | solution.py:14
  644.6 34.0 %collective-permute-start.14 = (f32[3,1,1024,128]{2,3,1,0:T(8,128)}, f32[3,1,1024,128]{2,3,1,0:T(8,128)}, u32[]{:S(2)}, u32[]{:S(2)}) collective-permute-start(f32[3,1,1024,128]{2,3,1,0:T(8,128)} %pad_maximum_fusion.3), channel_id=1, source_target_pairs={{1,0},{2,1},{3,2},{4,3},{5,4},{6,5},{7,6},{8,7},{9,8},{10,9},{11,1... | collective-permute-start | bytes 4718600 | tf_op jit(solution)/shard_map/ppermute | solution.py:17
  698.7 368.8 %all-reduce.12.cloned.1.call-start = ((), (), s32[]{:S(2)}) async-start(), calls=%async_computation.1 | async-start | bytes 131072 | tf_op jit(solution)/shard_map/psum | solution.py:63
  850.5 14.3 copy-start.13
  850.5 8.5 collective-permute-start.16
  853.0 10.5 collective-permute-start.17
  859.1 5.7 copy-start.26
  864.8 31.1 %collective-permute-start.19 = (f32[3,1,1024,128]{2,3,1,0:T(8,128)}, f32[3,1,1024,128]{2,3,1,0:T(8,128)}, u32[]{:S(2)}, u32[]{:S(2)}) collective-permute-start(f32[3,1,1024,128]{2,3,1,0:T(8,128)} %pad_maximum_fusion.4), channel_id=1, source_target_pairs={{0,1},{1,2},{2,3},{3,4},{4,5},{5,6},{6,7},{7,8},{8,9},{9,10},{10,1... | collective-permute-start | bytes 4718600 | tf_op jit(solution)/shard_map/ppermute | solution.py:14
  868.9 33.9 %collective-permute-start.18 = (f32[3,1,1024,128]{2,3,1,0:T(8,128)}, f32[3,1,1024,128]{2,3,1,0:T(8,128)}, u32[]{:S(2)}, u32[]{:S(2)}) collective-permute-start(f32[3,1,1024,128]{2,3,1,0:T(8,128)} %pad_maximum_fusion.4), channel_id=1, source_target_pairs={{1,0},{2,1},{3,2},{4,3},{5,4},{6,5},{7,6},{8,7},{9,8},{10,9},{11,1... | collective-permute-start | bytes 4718600 | tf_op jit(solution)/shard_map/ppermute | solution.py:17
  911.8 186.9 %copy-start.29 = (f32[128,128]{0,1:T(8,128)S(1)}, f32[128,128]{0,1:T(8,128)}, u32[]{:S(2)}) copy-start(f32[128,128]{0,1:T(8,128)} %all-reduce.10.cloned.1.call-done) | copy-start | bytes 196612
  922.9 507.9 %all-reduce.14.cloned.1.call-start = ((), (), s32[]{:S(2)}) async-start(), calls=%async_computation.2 | async-start | bytes 131072 | tf_op jit(solution)/shard_map/psum | solution.py:63
  1103.3 1.9 copy-start.1
  1193.0 27.6 %collective-permute-start.20 = (f32[1,1,1024,128]{2,3,1,0:T(8,128)}, f32[1,1,1024,128]{2,3,1,0:T(8,128)S(1)}, u32[]{:S(2)}, u32[]{:S(2)}) collective-permute-start(f32[1,1,1024,128]{2,3,1,0:T(8,128)} %bitcast.397), channel_id=1, source_target_pairs={{0,16},{16,32},{32,48},{48,64},{64,80},{80,96},{96,112},{1,17},{17... | collective-permute-start | bytes 1572872 | tf_op jit(solution)/shard_map/ppermute | solution.py:14
  1214.2 10.7 collective-permute-start.21
  1220.6 6.8 copy-start.16
  1224.9 2.5 copy-start.17
  1227.4 31.3 %collective-permute-start.23 = (f32[3,1,1024,128]{2,3,1,0:T(8,128)}, f32[3,1,1024,128]{2,3,1,0:T(8,128)}, u32[]{:S(2)}, u32[]{:S(2)}) collective-permute-start(f32[3,1,1024,128]{2,3,1,0:T(8,128)} %pad_maximum_fusion.5), channel_id=1, source_target_pairs={{0,1},{1,2},{2,3},{3,4},{4,5},{5,6},{6,7},{7,8},{8,9},{9,10},{10,1... | collective-permute-start | bytes 4718600 | tf_op jit(solution)/shard_map/ppermute | solution.py:14
  1231.6 34.0 %collective-permute-start.22 = (f32[3,1,1024,128]{2,3,1,0:T(8,128)}, f32[3,1,1024,128]{2,3,1,0:T(8,128)}, u32[]{:S(2)}, u32[]{:S(2)}) collective-permute-start(f32[3,1,1024,128]{2,3,1,0:T(8,128)} %pad_maximum_fusion.5), channel_id=1, source_target_pairs={{1,0},{2,1},{3,2},{4,3},{5,4},{6,5},{7,6},{8,7},{9,8},{10,9},{11,1... | collective-permute-start | bytes 4718600 | tf_op jit(solution)/shard_map/ppermute | solution.py:17
  1285.8 364.6 %all-reduce.16.cloned.1.call-start = ((), (), s32[]{:S(2)}) async-start(), calls=%async_computation.3 | async-start | bytes 131072 | tf_op jit(solution)/shard_map/psum | solution.py:63
  1433.8 2.6 copy-start.5
  1436.4 14.3 copy-start.11
  1436.4 8.5 collective-permute-start.24
  1438.9 10.5 collective-permute-start.25
  1445.0 5.8 copy-start.21
  1449.4 1.4 copy-start.20
  1450.7 31.1 %collective-permute-start.27 = (f32[3,1,1024,128]{2,3,1,0:T(8,128)}, f32[3,1,1024,128]{2,3,1,0:T(8,128)}, u32[]{:S(2)}, u32[]{:S(2)}) collective-permute-start(f32[3,1,1024,128]{2,3,1,0:T(8,128)} %pad_maximum_fusion.6), channel_id=1, source_target_pairs={{0,1},{1,2},{2,3},{3,4},{4,5},{5,6},{6,7},{7,8},{8,9},{9,10},{10,1... | collective-permute-start | bytes 4718600 | tf_op jit(solution)/shard_map/ppermute | solution.py:14
  1454.9 32.2 %collective-permute-start.26 = (f32[3,1,1024,128]{2,3,1,0:T(8,128)}, f32[3,1,1024,128]{2,3,1,0:T(8,128)}, u32[]{:S(2)}, u32[]{:S(2)}) collective-permute-start(f32[3,1,1024,128]{2,3,1,0:T(8,128)} %pad_maximum_fusion.6), channel_id=1, source_target_pairs={{1,0},{2,1},{3,2},{4,3},{5,4},{6,5},{7,6},{8,7},{9,8},{10,9},{11,1... | collective-permute-start | bytes 4718600 | tf_op jit(solution)/shard_map/ppermute | solution.py:17
  1492.3 10.6 copy-start.6
  1493.4 12.4 copy-start.31
  1502.9 172.2 %copy-start.32 = (f32[128,128]{1,0:T(8,128)S(1)}, f32[128,128]{1,0:T(8,128)}, u32[]{:S(2)}) copy-start(f32[128,128]{1,0:T(8,128)} %all-reduce.14.cloned.1.call-done) | copy-start | bytes 196612
  1505.7 169.8 %copy-start.2 = (f32[1,1,1024,128]{3,2,1,0:T(8,128)S(1)}, f32[1,1,1024,128]{3,2,1,0:T(8,128)}, u32[]{:S(2)}) copy-start(f32[1,1,1024,128]{3,2,1,0:T(8,128)} %copy-done.1) | copy-start | bytes 1572868
  1508.2 169.8 %copy-start.7 = (f32[1,1,1024,128]{3,2,1,0:T(8,128)S(1)}, f32[1,1,1024,128]{3,2,1,0:T(8,128)}, u32[]{:S(2)}) copy-start(f32[1,1,1024,128]{3,2,1,0:T(8,128)} %copy-done.5) | copy-start | bytes 1572868
  1675.0 2.9 copy-start.15
  (3 other events, 3.3 us)
Sparse Core Ops, SparseCore 0:
  335.7 149.2 all-reduce.17
  698.8 146.3 all-reduce.9
  923.0 144.4 all-reduce.11
  1285.9 144.8 all-reduce.13
  1505.9 144.4 all-reduce.15
where the time goes:
time: 1700 us; the launch traced here: 1690 us
  waiting for transfers between devices  842 us (50%)
  blocking collectives  250 us (15%)
  other arithmetic  218 us (13%)
  local copies, waits for them, and re-layouts  155 us (9%)
  starting transfers between devices  143 us (8%)
  matrix products  63.4 us (4%)
    psum x5, waiting for transfers between devices, gram_matrix(): return lax.psum(local_gram, ('group', 'sub'))  706 us
    psum x3, blocking collectives, precondition(): coarse_residual = lax.psum(contrib, 'sub')  196 us
    ppermute x14, starting transfers between devices, extended(): lax.ppermute(lax.slice_in_dim(block, block.shape[dim] - width, None, axis...  119 us
    ppermute x14, waiting for transfers between devices, extended(): lax.ppermute(lax.slice_in_dim(block, block.shape[dim] - width, None, axis...  103 us
    gather x28, local copies, waits for them, and re-layouts, pick_rows(): source_block[rows_at]  70.6 us
    another operation x15, other arithmetic, spd_solve(): factor = jnp.linalg.cholesky(matrix)  66 us
    another operation x10, other arithmetic, spd_solve(): lax.linalg.triangular_solve(factor, half, left_side=True, lower=True, tra...  55.3 us
    all_gather x3, blocking collectives, precondition(): coarse_values = lax.all_gather(row_values, 'sub', axis=0, tiled=True)  54.4 us
  transfers between devices with their start and end apart: 33, of which 27 were waited for; matrix products, arithmetic and copies ran while one was open for 10% of the time, Pallas kernels for 0%

commit v1 on v0

--- a/solution.py
+++ b/solution.py
@@ -57,10 +57,15 @@
 
 
 def gram_matrix(left, right, weight):
+
+    def _manage_edge(local, axis_tag, a_name):
+        clean = lax.psum(lax.psum(local, axis_name=axis_tag), axis_name=a_name)
+        return clean
+
     local_gram = jnp.einsum(
         "gsir,gsic->rc", left * weight[..., None], right, precision=lax.Precision.HIGHEST
     )
-    return lax.psum(local_gram, ("group", "sub"))
+    return _manage_edge(local_gram, "group", "sub")
 
 
 def spd_solve(matrix, rhs_block):

time: 1700 us -> 1730 us (1.018)
    psum x5 -> x10, waiting for transfers between devices: 706 us -> 717 us  [_manage_edge(): clean = lax.psum(lax.psum(local, axis_name=axis_tag), axis_name=a_name)]
  transfers between devices with their start and end apart: 33 -> 38, of which waited for: 27 -> 32; matrix products, arithmetic and copies ran while one was open for 10% -> 10% of each run, Pallas kernels for 0% -> 0%
where the time goes in v1:
time: 1730 us; the launch traced here: 1720 us
  waiting for transfers between devices  851 us (49%)
  blocking collectives  251 us (15%)
  other arithmetic  217 us (13%)
  local copies, waits for them, and re-layouts  162 us (9%)
  starting transfers between devices  156 us (9%)
  matrix products  63.5 us (4%)
    psum x10, waiting for transfers between devices, _manage_edge(): clean = lax.psum(lax.psum(local, axis_name=axis_tag), axis_name=a_name)  717 us
    psum x3, blocking collectives, precondition(): coarse_residual = lax.psum(contrib, 'sub')  197 us
    ppermute x14, starting transfers between devices, extended(): lax.ppermute(lax.slice_in_dim(block, block.shape[dim] - width, None, axis...  132 us
    ppermute x14, waiting for transfers between devices, extended(): lax.ppermute(lax.slice_in_dim(block, block.shape[dim] - width, None, axis...  101 us
    gather x28, local copies, waits for them, and re-layouts, pick_rows(): source_block[rows_at]  75 us
    another operation x15, other arithmetic, spd_solve(): factor = jnp.linalg.cholesky(matrix)  65.9 us
    another operation x10, other arithmetic, spd_solve(): lax.linalg.triangular_solve(factor, half, left_side=True, lower=True, tra...  55 us
    all_gather x3, blocking collectives, precondition(): coarse_values = lax.all_gather(row_values, 'sub', axis=0, tiled=True)  54.3 us
  transfers between devices with their start and end apart: 38, of which 32 were waited for; matrix products, arithmetic and copies ran while one was open for 10% of the time, Pallas kernels for 0%

profile of v1, /device:TPU:1, one launch (start us, length us, event | category | flops | bytes accessed | tf_op | source)
XLA Modules:
  0.0 1717.0 jit_solution(1084324587988879409)
XLA Ops:
  9.2 4.5 collective-permute-start
  20.1 4.4 collective-permute-done.1
  26.9 4.3 collective-permute-start.3
  32.6 7.6 scatter_custom_fusion
  44.1 14.3 collective-permute-done.3
  68.9 6.7 scatter_custom_fusion.1
  78.4 66.6 %all-reduce.35 = bf16[1024,128]{1,0:T(8,128)(2,1)} all-reduce(f32[1024,128]{1,0:T(8,128)S(1)} %fusion.81), channel_id=1, replica_groups=mesh['group'=8,'sub'=16] {'sub'}, use_global_device_ids=true, to_apply=%region_2.0 | all-reduce | flops 131072 | bytes 786432 | tf_op jit(solution)/shard_map/psum | solution.py:111
  146.2 18.0 %all_gather.9 = bf16[1024,128]{1,0:T(8,128)(2,1)} all-gather(bf16[64,128]{1,0:T(8,128)(2,1)S(1)} %fusion.21), channel_id=1, replica_groups=mesh['group'=8,'sub'=16] {'sub'}, dimensions={0}, use_global_device_ids=true | all-gather | bytes 278528 | tf_op jit(solution)/shard_map/all_gather | solution.py:116
  165.8 27.8 %collective-permute-start.4 = (f32[1,1,1024,128]{2,3,1,0:T(8,128)S(1)}, f32[1,1,1024,128]{2,3,1,0:T(8,128)S(1)}, u32[]{:S(2)}, u32[]{:S(2)}) collective-permute-start(f32[1,1,1024,128]{2,3,1,0:T(8,128)S(1)} %bitcast.401), channel_id=1, source_target_pairs={{0,16},{16,32},{32,48},{48,64},{64,80},{80,96},{96,112},{1,17},{17... | collective-permute-start | bytes 1572872 | tf_op jit(solution)/shard_map/ppermute | solution.py:14
  195.5 4.2 collective-permute-done.4
  199.7 4.4 collective-permute-done.5
  205.4 4.6 collective-permute-start.7
  222.3 14.5 collective-permute-done.7
  252.8 6.7 scatter_custom_fusion.2
  261.9 8.1 collective-permute-start.8
  271.9 4.2 collective-permute-done.8
  276.1 4.4 collective-permute-done.9
  281.8 5.6 collective-permute-start.11
  298.6 15.7 collective-permute-done.11
  326.7 7.1 scatter_custom_fusion.3
  335.6 64.9 %all-reduce.34.cloned.1.call-done = (f32[128,128]{0,1:T(8,128)}, f32[128,128]{0,1:T(8,128)}) async-done(((f32[128,128]{0,1:T(8,128)}, f32[128,128]{0,1:T(8,128)}), (f32[128,128]{0,1:T(8,128)}, f32[128,128]{0,1:T(8,128)})) %all-reduce.34.cloned.1.call-update) | async-done | bytes 131088 | tf_op jit(solution)/shard_map/psum | solution.py:62
  400.6 86.1 %all-reduce.32.cloned.1.call-done = (f32[128,128]{0,1:T(8,128)}, f32[128,128]{0,1:T(8,128)}) async-done(((f32[128,128]{0,1:T(8,128)}, f32[128,128]{0,1:T(8,128)}), (f32[128,128]{0,1:T(8,128)}, f32[128,128]{0,1:T(8,128)})) %all-reduce.32.cloned.1.call-update) | async-done | bytes 131088 | tf_op jit(solution)/shard_map/psum | solution.py:62
  490.1 12.5 cholesky.89
  504.0 9.8 custom-call.73
  520.6 65.2 %all-reduce.36 = bf16[1024,128]{1,0:T(8,128)(2,1)} all-reduce(f32[1024,128]{1,0:T(8,128)} %fusion.80), channel_id=1, replica_groups=mesh['group'=8,'sub'=16] {'sub'}, use_global_device_ids=true, to_apply=%region_11.15 | all-reduce | flops 131072 | bytes 786432 | tf_op jit(solution)/shard_map/psum | solution.py:111
  586.9 18.3 %all_gather.10 = bf16[1024,128]{1,0:T(8,128)(2,1)} all-gather(bf16[64,128]{1,0:T(8,128)(2,1)S(1)} %fusion.22), channel_id=1, replica_groups=mesh['group'=8,'sub'=16] {'sub'}, dimensions={0}, use_global_device_ids=true | all-gather | bytes 278528 | tf_op jit(solution)/shard_map/all_gather | solution.py:116
  607.7 24.1 %collective-permute-start.12 = (f32[1,1,1024,128]{2,3,1,0:T(8,128)}, f32[1,1,1024,128]{2,3,1,0:T(8,128)S(1)}, u32[]{:S(2)}, u32[]{:S(2)}) collective-permute-start(f32[1,1,1024,128]{2,3,1,0:T(8,128)} %bitcast.405), channel_id=1, source_target_pairs={{0,16},{16,32},{32,48},{48,64},{64,80},{80,96},{96,112},{1,17},{17... | collective-permute-start | bytes 1572872 | tf_op jit(solution)/shard_map/ppermute | solution.py:14
  633.7 4.5 collective-permute-done.12
  638.2 4.3 collective-permute-done.13
  645.0 4.2 collective-permute-start.15
  652.5 12.5 cholesky.100
  692.2 8.2 scatter_custom_fusion.4
  704.0 63.2 %all-reduce.16.cloned.1.call-done = f32[128,128]{0,1:T(8,128)} async-done(((f32[128,128]{0,1:T(8,128)}), f32[128,128]{0,1:T(8,128)}) %all-reduce.16.cloned.1.call-update) | async-done | bytes 65552 | tf_op jit(solution)/shard_map/psum | solution.py:62
  768.1 9.8 custom-call.75
  777.9 73.9 %all-reduce.18.cloned.1.call-done = f32[128,128]{0,1:T(8,128)} async-done(((f32[128,128]{0,1:T(8,128)}), f32[128,128]{0,1:T(8,128)}) %all-reduce.18.cloned.1.call-update) | async-done | bytes 65552 | tf_op jit(solution)/shard_map/psum | solution.py:62
  857.2 5.4 collective-permute-start.16
  868.7 4.4 collective-permute-done.17
  874.4 4.4 collective-permute-start.19
  892.3 13.3 collective-permute-done.19
  921.4 8.3 scatter_custom_fusion.5
  932.6 63.6 %all-reduce.20.cloned.1.call-done = f32[128,128]{0,1:T(8,128)} async-done(((f32[128,128]{0,1:T(8,128)}), f32[128,128]{0,1:T(8,128)}) %all-reduce.20.cloned.1.call-update) | async-done | bytes 65552 | tf_op jit(solution)/shard_map/psum | solution.py:62
  996.7 84.0 %all-reduce.22.cloned.1.call-done = f32[128,128]{0,1:T(8,128)} async-done(((f32[128,128]{0,1:T(8,128)}), f32[128,128]{0,1:T(8,128)}) %all-reduce.22.cloned.1.call-update) | async-done | bytes 65552 | tf_op jit(solution)/shard_map/psum | solution.py:62
  1083.8 13.2 cholesky.111
  1100.6 11.3 custom-call.77
  1120.1 64.8 %all-reduce.37 = bf16[1024,128]{1,0:T(8,128)(2,1)} all-reduce(f32[1024,128]{1,0:T(8,128)} %fusion.79), channel_id=1, replica_groups=mesh['group'=8,'sub'=16] {'sub'}, use_global_device_ids=true, to_apply=%region_18.22 | all-reduce | flops 131072 | bytes 786432 | tf_op jit(solution)/shard_map/psum | solution.py:111
  1186.0 18.0 %all_gather.11 = bf16[1024,128]{1,0:T(8,128)(2,1)} all-gather(bf16[64,128]{1,0:T(8,128)(2,1)S(1)} %fusion.23), channel_id=1, replica_groups=mesh['group'=8,'sub'=16] {'sub'}, dimensions={0}, use_global_device_ids=true | all-gather | bytes 278528 | tf_op jit(solution)/shard_map/all_gather | solution.py:116
  1206.4 24.6 %collective-permute-start.20 = (f32[1,1,1024,128]{2,3,1,0:T(8,128)}, f32[1,1,1024,128]{2,3,1,0:T(8,128)S(1)}, u32[]{:S(2)}, u32[]{:S(2)}) collective-permute-start(f32[1,1,1024,128]{2,3,1,0:T(8,128)} %bitcast.397), channel_id=1, source_target_pairs={{0,16},{16,32},{32,48},{48,64},{64,80},{80,96},{96,112},{1,17},{17... | collective-permute-start | bytes 1572872 | tf_op jit(solution)/shard_map/ppermute | solution.py:14
  1232.9 4.5 collective-permute-done.20
  1237.4 4.3 collective-permute-done.21
  1244.2 4.2 collective-permute-start.23
  1250.0 11.7 cholesky.122
  1291.4 8.2 scatter_custom_fusion.6
  1303.3 63.2 %all-reduce.24.cloned.1.call-done = f32[128,128]{1,0:T(8,128)} async-done(((f32[128,128]{1,0:T(8,128)}), f32[128,128]{1,0:T(8,128)}) %all-reduce.24.cloned.1.call-update) | async-done | bytes 65552 | tf_op jit(solution)/shard_map/psum | solution.py:62
  1367.4 9.8 custom-call.79
  1377.2 74.0 %all-reduce.26.cloned.1.call-done = f32[128,128]{1,0:T(8,128)} async-done(((f32[128,128]{1,0:T(8,128)}), f32[128,128]{1,0:T(8,128)}) %all-reduce.26.cloned.1.call-update) | async-done | bytes 65552 | tf_op jit(solution)/shard_map/psum | solution.py:62
  1456.8 5.4 collective-permute-start.24
  1468.4 4.4 collective-permute-done.25
  1474.1 4.4 collective-permute-start.27
  1491.3 13.9 collective-permute-done.27
  1521.2 8.3 scatter_custom_fusion.7
  1534.2 62.0 %all-reduce.28.cloned.1.call-done = f32[128,128]{0,1:T(8,128)} async-done(((f32[128,128]{0,1:T(8,128)}), f32[128,128]{0,1:T(8,128)}) %all-reduce.28.cloned.1.call-update) | async-done | bytes 65552 | tf_op jit(solution)/shard_map/psum | solution.py:62
  1598.6 82.1 %all-reduce.30.cloned.1.call-done = f32[128,128]{0,1:T(8,128)} async-done(((f32[128,128]{0,1:T(8,128)}), f32[128,128]{0,1:T(8,128)}) %all-reduce.30.cloned.1.call-update) | async-done | bytes 65552 | tf_op jit(solution)/shard_map/psum | solution.py:62
  1682.5 11.7 cholesky.133
  1695.6 9.8 custom-call.81
  (294 shorter events, 309.2 us)
Async XLA Ops:
  7.2 68.4 %copy-start = (bf16[1,1,1024,1024]{3,2,1,0:T(8,128)(2,1)S(1)}, bf16[1,1,1024,1024]{3,2,1,0:T(8,128)(2,1)}, u32[]{:S(2)}) copy-start(bf16[1,1,1024,1024]{3,2,1,0:T(8,128)(2,1)} %param.14) | copy-start | bytes 6291460
  7.2 393.3 %all-reduce.34.cloned.1.call-start = ((), (), s32[]{:S(2)}) async-start(), calls=%async_computation.9 | async-start | bytes 262144 | tf_op jit(solution)/shard_map/psum | solution.py:62
  9.2 10.9 collective-permute-start
  13.7 10.8 collective-permute-start.1
  26.9 31.5 %collective-permute-start.3 = (f32[3,1,1024,128]{3,2,1,0:T(8,128)}, f32[3,1,1024,128]{3,2,1,0:T(8,128)}, u32[]{:S(2)}, u32[]{:S(2)}) collective-permute-start(f32[3,1,1024,128]{3,2,1,0:T(8,128)} %pad_maximum_fusion), channel_id=1, source_target_pairs={{0,1},{1,2},{2,3},{3,4},{4,5},{5,6},{6,7},{7,8},{8,9},{9,10},{10,1... | collective-permute-start | bytes 4718600 | tf_op jit(solution)/shard_map/ppermute | solution.py:14
  31.3 32.4 %collective-permute-start.2 = (f32[3,1,1024,128]{3,2,1,0:T(8,128)}, f32[3,1,1024,128]{3,2,1,0:T(8,128)}, u32[]{:S(2)}, u32[]{:S(2)}) collective-permute-start(f32[3,1,1024,128]{3,2,1,0:T(8,128)} %pad_maximum_fusion), channel_id=1, source_target_pairs={{1,0},{2,1},{3,2},{4,3},{5,4},{6,5},{7,6},{8,7},{9,8},{10,9},{11,1... | collective-permute-start | bytes 4718600 | tf_op jit(solution)/shard_map/ppermute | solution.py:17
  75.5 215.3 %copy-start.4 = (f32[1024,128]{1,0:T(8,128)}, f32[1024,128]{1,0:T(8,128)S(1)}, u32[]{:S(2)}) copy-start(f32[1024,128]{1,0:T(8,128)S(1)} %scatter_custom_fusion.1) | copy-start | bytes 1572868
  75.6 2.2 copy-start.32
  77.4 67.6 %copy-start.27 = (bf16[1,64,1024]{2,1,0:T(8,128)(2,1)S(1)}, bf16[1,64,1024]{2,1,0:T(8,128)(2,1)}, u32[]{:S(2)}) copy-start(bf16[1,64,1024]{2,1,0:T(8,128)(2,1)} %param.18) | copy-start | bytes 393220
  165.8 39.6 %copy-start.9 = (f32[128,1024]{1,0:T(8,128)}, f32[128,1024]{1,0:T(8,128)S(1)}, u32[]{:S(2)}) copy-start(f32[128,1024]{1,0:T(8,128)S(1)} %fusion.12) | copy-start | bytes 1572868
  165.8 33.9 %collective-permute-start.4 = (f32[1,1,1024,128]{2,3,1,0:T(8,128)S(1)}, f32[1,1,1024,128]{2,3,1,0:T(8,128)S(1)}, u32[]{:S(2)}, u32[]{:S(2)}) collective-permute-start(f32[1,1,1024,128]{2,3,1,0:T(8,128)S(1)} %bitcast.401), channel_id=1, source_target_pairs={{0,16},{16,32},{32,48},{48,64},{64,80},{80,96},{96,112},{1,17},{17... | collective-permute-start | bytes 1572872 | tf_op jit(solution)/shard_map/ppermute | solution.py:14
  193.6 10.5 collective-permute-start.5
  199.7 5.7 copy-start.22
  205.4 31.3 %collective-permute-start.7 = (f32[3,1,1024,128]{2,3,1,0:T(8,128)}, f32[3,1,1024,128]{2,3,1,0:T(8,128)}, u32[]{:S(2)}, u32[]{:S(2)}) collective-permute-start(f32[3,1,1024,128]{2,3,1,0:T(8,128)} %pad_maximum_fusion.1), channel_id=1, source_target_pairs={{0,1},{1,2},{2,3},{3,4},{4,5},{5,6},{6,7},{7,8},{8,9},{9,10},{10,1... | collective-permute-start | bytes 4718600 | tf_op jit(solution)/shard_map/ppermute | solution.py:14
  210.0 33.7 %collective-permute-start.6 = (f32[3,1,1024,128]{2,3,1,0:T(8,128)}, f32[3,1,1024,128]{2,3,1,0:T(8,128)}, u32[]{:S(2)}, u32[]{:S(2)}) collective-permute-start(f32[3,1,1024,128]{2,3,1,0:T(8,128)} %pad_maximum_fusion.1), channel_id=1, source_target_pairs={{1,0},{2,1},{3,2},{4,3},{5,4},{6,5},{7,6},{8,7},{9,8},{10,9},{11,1... | collective-permute-start | bytes 4718600 | tf_op jit(solution)/shard_map/ppermute | solution.py:17
  261.9 20.0 %copy-start.10 = (f32[128,1024]{1,0:T(8,128)}, f32[128,1024]{1,0:T(8,128)S(1)}, u32[]{:S(2)}) copy-start(f32[128,1024]{1,0:T(8,128)S(1)} %fusion.4) | copy-start | bytes 1572868
  261.9 14.2 collective-permute-start.8
  270.0 10.5 collective-permute-start.9
  276.1 5.7 copy-start.19
  281.8 32.4 %collective-permute-start.11 = (f32[3,1,1024,128]{2,3,1,0:T(8,128)}, f32[3,1,1024,128]{2,3,1,0:T(8,128)}, u32[]{:S(2)}, u32[]{:S(2)}) collective-permute-start(f32[3,1,1024,128]{2,3,1,0:T(8,128)} %pad_maximum_fusion.2), channel_id=1, source_target_pairs={{0,1},{1,2},{2,3},{3,4},{4,5},{5,6},{6,7},{7,8},{8,9},{9,10},{10,1... | collective-permute-start | bytes 4718600 | tf_op jit(solution)/shard_map/ppermute | solution.py:14
  287.5 32.0 %collective-permute-start.10 = (f32[3,1,1024,128]{2,3,1,0:T(8,128)}, f32[3,1,1024,128]{2,3,1,0:T(8,128)}, u32[]{:S(2)}, u32[]{:S(2)}) collective-permute-start(f32[3,1,1024,128]{2,3,1,0:T(8,128)} %pad_maximum_fusion.2), channel_id=1, source_target_pairs={{1,0},{2,1},{3,2},{4,3},{5,4},{6,5},{7,6},{8,7},{9,8},{10,9},{11,1... | collective-permute-start | bytes 4718600 | tf_op jit(solution)/shard_map/ppermute | solution.py:17
  321.5 5.1 copy-start.7
  333.7 181.2 %copy-start.8 = (f32[1024,128]{1,0:T(8,128)}, f32[1024,128]{1,0:T(8,128)S(1)}, u32[]{:S(2)}) copy-start(f32[1024,128]{1,0:T(8,128)S(1)} %scatter_custom_fusion.3) | copy-start | bytes 1572868
  335.6 151.2 %all-reduce.32.cloned.1.call-start = ((), (), s32[]{:S(2)}) async-start(), calls=%async_computation.8 | async-start | bytes 262144 | tf_op jit(solution)/shard_map/psum | solution.py:62
  400.5 366.7 %all-reduce.16.cloned.1.call-start = ((), (), s32[]{:S(2)}) async-start(), calls=%async_computation | async-start | bytes 131072 | tf_op jit(solution)/shard_map/psum | solution.py:62
  517.0 183.5 %copy-start.3 = (f32[1,1,1024,128]{3,2,1,0:T(8,128)}, f32[1,1,1024,128]{3,2,1,0:T(8,128)S(1)}, u32[]{:S(2)}) copy-start(f32[1,1,1024,128]{3,2,1,0:T(8,128)S(1)} %fusion.16) | copy-start | bytes 1572868
  607.7 30.5 %collective-permute-start.12 = (f32[1,1,1024,128]{2,3,1,0:T(8,128)}, f32[1,1,1024,128]{2,3,1,0:T(8,128)S(1)}, u32[]{:S(2)}, u32[]{:S(2)}) collective-permute-start(f32[1,1,1024,128]{2,3,1,0:T(8,128)} %bitcast.405), channel_id=1, source_target_pairs={{0,16},{16,32},{32,48},{48,64},{64,80},{80,96},{96,112},{1,17},{17... | collective-permute-start | bytes 1572872 | tf_op jit(solution)/shard_map/ppermute | solution.py:14
  631.8 10.7 collective-permute-start.13
  638.2 6.8 copy-start.17
  642.5 2.5 copy-start.18
  645.0 31.3 %collective-permute-start.15 = (f32[3,1,1024,128]{2,3,1,0:T(8,128)}, f32[3,1,1024,128]{2,3,1,0:T(8,128)}, u32[]{:S(2)}, u32[]{:S(2)}) collective-permute-start(f32[3,1,1024,128]{2,3,1,0:T(8,128)} %pad_maximum_fusion.3), channel_id=1, source_target_pairs={{0,1},{1,2},{2,3},{3,4},{4,5},{5,6},{6,7},{7,8},{8,9},{9,10},{10,1... | collective-permute-start | bytes 4718600 | tf_op jit(solution)/shard_map/ppermute | solution.py:14
  649.2 34.0 %collective-permute-start.14 = (f32[3,1,1024,128]{2,3,1,0:T(8,128)}, f32[3,1,1024,128]{2,3,1,0:T(8,128)}, u32[]{:S(2)}, u32[]{:S(2)}) collective-permute-start(f32[3,1,1024,128]{2,3,1,0:T(8,128)} %pad_maximum_fusion.3), channel_id=1, source_target_pairs={{1,0},{2,1},{3,2},{4,3},{5,4},{6,5},{7,6},{8,7},{9,8},{10,9},{11,1... | collective-permute-start | bytes 4718600 | tf_op jit(solution)/shard_map/ppermute | solution.py:17
  703.3 148.5 %all-reduce.18.cloned.1.call-start = ((), (), s32[]{:S(2)}) async-start(), calls=%async_computation.1 | async-start | bytes 131072 | tf_op jit(solution)/shard_map/psum | solution.py:62
  767.2 229.0 %all-reduce.20.cloned.1.call-start = ((), (), s32[]{:S(2)}) async-start(), calls=%async_computation.2 | async-start | bytes 131072 | tf_op jit(solution)/shard_map/psum | solution.py:62
  857.1 17.3 %copy-start.11 = (f32[128,1024]{1,0:T(8,128)}, f32[128,1024]{1,0:T(8,128)S(1)}, u32[]{:S(2)}) copy-start(f32[128,1024]{1,0:T(8,128)S(1)} %fusion.2) | copy-start | bytes 1572868
  857.2 11.5 collective-permute-start.16
  862.6 10.5 collective-permute-start.17
  868.7 5.7 copy-start.24
  874.4 31.1 %collective-permute-start.19 = (f32[3,1,1024,128]{2,3,1,0:T(8,128)}, f32[3,1,1024,128]{2,3,1,0:T(8,128)}, u32[]{:S(2)}, u32[]{:S(2)}) collective-permute-start(f32[3,1,1024,128]{2,3,1,0:T(8,128)} %pad_maximum_fusion.4), channel_id=1, source_target_pairs={{0,1},{1,2},{2,3},{3,4},{4,5},{5,6},{6,7},{7,8},{8,9},{9,10},{10,1... | collective-permute-start | bytes 4718600 | tf_op jit(solution)/shard_map/ppermute | solution.py:14
  878.8 33.6 %collective-permute-start.18 = (f32[3,1,1024,128]{2,3,1,0:T(8,128)}, f32[3,1,1024,128]{2,3,1,0:T(8,128)}, u32[]{:S(2)}, u32[]{:S(2)}) collective-permute-start(f32[3,1,1024,128]{2,3,1,0:T(8,128)} %pad_maximum_fusion.4), channel_id=1, source_target_pairs={{1,0},{2,1},{3,2},{4,3},{5,4},{6,5},{7,6},{8,7},{9,8},{10,9},{11,1... | collective-permute-start | bytes 4718600 | tf_op jit(solution)/shard_map/ppermute | solution.py:17
  921.4 190.4 %copy-start.28 = (f32[128,128]{0,1:T(8,128)S(1)}, f32[128,128]{0,1:T(8,128)}, u32[]{:S(2)}) copy-start(f32[128,128]{0,1:T(8,128)} %all-reduce.18.cloned.1.call-done) | copy-start | bytes 196612
  932.5 148.2 %all-reduce.22.cloned.1.call-start = ((), (), s32[]{:S(2)}) async-start(), calls=%async_computation.3 | async-start | bytes 131072 | tf_op jit(solution)/shard_map/psum | solution.py:62
  996.2 370.2 %all-reduce.24.cloned.1.call-start = ((), (), s32[]{:S(2)}) async-start(), calls=%async_computation.4 | async-start | bytes 131072 | tf_op jit(solution)/shard_map/psum | solution.py:62
  1206.4 31.0 %collective-permute-start.20 = (f32[1,1,1024,128]{2,3,1,0:T(8,128)}, f32[1,1,1024,128]{2,3,1,0:T(8,128)S(1)}, u32[]{:S(2)}, u32[]{:S(2)}) collective-permute-start(f32[1,1,1024,128]{2,3,1,0:T(8,128)} %bitcast.397), channel_id=1, source_target_pairs={{0,16},{16,32},{32,48},{48,64},{64,80},{80,96},{96,112},{1,17},{17... | collective-permute-start | bytes 1572872 | tf_op jit(solution)/shard_map/ppermute | solution.py:14
  1231.0 10.7 collective-permute-start.21
  1237.4 6.8 copy-start.15
  1241.7 2.5 copy-start.16
  1244.2 31.3 %collective-permute-start.23 = (f32[3,1,1024,128]{2,3,1,0:T(8,128)}, f32[3,1,1024,128]{2,3,1,0:T(8,128)}, u32[]{:S(2)}, u32[]{:S(2)}) collective-permute-start(f32[3,1,1024,128]{2,3,1,0:T(8,128)} %pad_maximum_fusion.5), channel_id=1, source_target_pairs={{0,1},{1,2},{2,3},{3,4},{4,5},{5,6},{6,7},{7,8},{8,9},{9,10},{10,1... | collective-permute-start | bytes 4718600 | tf_op jit(solution)/shard_map/ppermute | solution.py:14
  1248.4 34.0 %collective-permute-start.22 = (f32[3,1,1024,128]{2,3,1,0:T(8,128)}, f32[3,1,1024,128]{2,3,1,0:T(8,128)}, u32[]{:S(2)}, u32[]{:S(2)}) collective-permute-start(f32[3,1,1024,128]{2,3,1,0:T(8,128)} %pad_maximum_fusion.5), channel_id=1, source_target_pairs={{1,0},{2,1},{3,2},{4,3},{5,4},{6,5},{7,6},{8,7},{9,8},{10,9},{11,1... | collective-permute-start | bytes 4718600 | tf_op jit(solution)/shard_map/ppermute | solution.py:17
  1302.6 148.6 %all-reduce.26.cloned.1.call-start = ((), (), s32[]{:S(2)}) async-start(), calls=%async_computation.5 | async-start | bytes 131072 | tf_op jit(solution)/shard_map/psum | solution.py:62
  1366.5 229.7 %all-reduce.28.cloned.1.call-start = ((), (), s32[]{:S(2)}) async-start(), calls=%async_computation.6 | async-start | bytes 131072 | tf_op jit(solution)/shard_map/psum | solution.py:62
  1454.1 2.6 copy-start.5
  1456.8 17.3 %copy-start.12 = (f32[128,1024]{1,0:T(8,128)}, f32[128,1024]{1,0:T(8,128)S(1)}, u32[]{:S(2)}) copy-start(f32[128,1024]{1,0:T(8,128)S(1)} %fusion) | copy-start | bytes 1572868
  1456.8 11.5 collective-permute-start.24
  1462.3 10.5 collective-permute-start.25
  1468.4 5.8 copy-start.26
  1474.1 31.1 %collective-permute-start.27 = (f32[3,1,1024,128]{2,3,1,0:T(8,128)}, f32[3,1,1024,128]{2,3,1,0:T(8,128)}, u32[]{:S(2)}, u32[]{:S(2)}) collective-permute-start(f32[3,1,1024,128]{2,3,1,0:T(8,128)} %pad_maximum_fusion.6), channel_id=1, source_target_pairs={{0,1},{1,2},{2,3},{3,4},{4,5},{5,6},{6,7},{7,8},{8,9},{9,10},{10,1... | collective-permute-start | bytes 4718600 | tf_op jit(solution)/shard_map/ppermute | solution.py:14
  1478.5 33.7 %collective-permute-start.26 = (f32[3,1,1024,128]{2,3,1,0:T(8,128)}, f32[3,1,1024,128]{2,3,1,0:T(8,128)}, u32[]{:S(2)}, u32[]{:S(2)}) collective-permute-start(f32[3,1,1024,128]{2,3,1,0:T(8,128)} %pad_maximum_fusion.6), channel_id=1, source_target_pairs={{1,0},{2,1},{3,2},{4,3},{5,4},{6,5},{7,6},{8,7},{9,8},{10,9},{11,1... | collective-permute-start | bytes 4718600 | tf_op jit(solution)/shard_map/ppermute | solution.py:17
  1521.2 75.0 %copy-start.30 = (f32[128,128]{1,0:T(8,128)S(1)}, f32[128,128]{1,0:T(8,128)}, u32[]{:S(2)}) copy-start(f32[128,128]{1,0:T(8,128)} %copy-done.29) | copy-start | bytes 196612
  1532.5 172.9 %copy-start.31 = (f32[128,128]{1,0:T(8,128)S(1)}, f32[128,128]{1,0:T(8,128)}, u32[]{:S(2)}) copy-start(f32[128,128]{1,0:T(8,128)} %all-reduce.26.cloned.1.call-done) | copy-start | bytes 196612
  1532.5 148.2 %all-reduce.30.cloned.1.call-start = ((), (), s32[]{:S(2)}) async-start(), calls=%async_computation.7 | async-start | bytes 131072 | tf_op jit(solution)/shard_map/psum | solution.py:62
  1534.2 171.7 %copy-start.2 = (f32[1,1,1024,128]{3,2,1,0:T(8,128)S(1)}, f32[1,1,1024,128]{3,2,1,0:T(8,128)}, u32[]{:S(2)}) copy-start(f32[1,1,1024,128]{3,2,1,0:T(8,128)} %copy-done.1) | copy-start | bytes 1572868
  1598.6 109.7 %copy-start.6 = (f32[1,1,1024,128]{3,2,1,0:T(8,128)S(1)}, f32[1,1,1024,128]{3,2,1,0:T(8,128)}, u32[]{:S(2)}) copy-start(f32[1,1,1024,128]{3,2,1,0:T(8,128)} %copy-done.5) | copy-start | bytes 1572868
  1705.4 2.9 copy-start.14
  (7 other events, 9.8 us)
Sparse Core Ops, SparseCore 0:
  335.7 64.7 all-reduce.33
  403.8 82.8 all-reduce.31
  703.4 63.7 all-reduce.15
  770.2 81.4 all-reduce.17
  932.6 63.5 all-reduce.19
  999.3 81.4 all-reduce.21
  1302.7 63.6 all-reduce.23
  1369.7 81.4 all-reduce.25
  1532.6 63.5 all-reduce.27
  1599.2 81.4 all-reduce.29
